TPU v7x, 256 devices: a whole 4x4x8 slice. The times are simulated.
256 devices in a mesh: hid: 4 (over x_lo, core), tok: 64 (over x_hi, y, z).
Axes of the slice: x: 4 (x_hi: 2, x_lo: 2; x = x_hi * 2 + x_lo), y: 4, z: 8, core: 2. Of those that a mesh axis runs over, the one named last changes fastest.
Arguments:
- val_inputs: bfloat16 [256, 4096], P(None, 'tok'), may hold values from -6 to 6
- val_out_grad: bfloat16 [256, 4096], P(None, 'tok'), may hold values from -6 to 6
- w_gate: bfloat16 [4096, 14336], P('tok', 'hid'), may hold values from -0.09375 to 0.09375
- w_up: bfloat16 [4096, 14336], P('tok', 'hid'), may hold values from -0.09375 to 0.09375
- w_down: bfloat16 [14336, 4096], P('hid', 'tok'), may hold values from -0.046875 to 0.046875
- val_attn_inputs: bfloat16 [256, 4096], P('hid', 'tok'), may hold values from -6 to 6
- train_inputs: bfloat16 [163840, 4096], P(('hid', 'tok')), may hold values from -6 to 6
- train_grads: bfloat16 [163840, 4096], P(('hid', 'tok')), may hold values from -6 to 6
Outputs:
- influence: float32 [163840], P(('hid', 'tok'))
- val_grad: bfloat16 [256, 4096], P('hid', 'tok')
All inputs are finite; a program needn't handle non-finite values.
Results may differ from a plain program's by a relative error of at most 0.0036.
Values may be sent and summed in bfloat16 or wider, within the bound.
No kernel may reach another device: no remote copies, remote signals or barrier semaphores. Data moves between devices by JAX's collectives and lax.ppermute only.
A program may use at most 128 MiB of HBM per device.

v0:
```python
import math
import jax
import jax.numpy as jnp
from jax import lax
from jax.sharding import PartitionSpec as P


def dot_rows(left, right):
    return lax.dot_general(
        left, right, (((1,), (1,)), ((), ())), preferred_element_type=jnp.float32
    )


def act_grads(gate_pre, up_pre, hid_grad):
    logistic = jax.nn.sigmoid(gate_pre)
    grad_gate = (hid_grad * up_pre * logistic * (1.0 + gate_pre * (1.0 - logistic))).astype(
        jnp.bfloat16
    )
    grad_up = (hid_grad * gate_pre * logistic).astype(jnp.bfloat16)
    return (grad_gate, grad_up)


def pair_terms(train_in, train_gr, val_in, val_gr):
    in_gram = dot_rows(train_in, val_in)
    grad_gram = dot_rows(train_gr, val_gr)
    return jnp.sum(in_gram * grad_gram, axis=1)


def local(
    val_inputs, val_out_grad, w_gate, w_up, w_down, val_attn_inputs, train_inputs, train_grads
):
    hid_units = w_gate.shape[1]
    val_count = val_out_grad.shape[0]
    gate_pre = jnp.dot(val_inputs, w_gate, preferred_element_type=jnp.float32)
    up_pre = jnp.dot(val_inputs, w_up, preferred_element_type=jnp.float32)
    hid_grad = dot_rows(val_out_grad, w_down)
    sums = lax.psum_scatter(
        jnp.concatenate([gate_pre, up_pre, hid_grad], axis=1),
        "tok",
        scatter_dimension=0,
        tiled=True,
    )
    grad_gate, grad_up = act_grads(
        sums[:, :hid_units], sums[:, hid_units : 2 * hid_units], sums[:, 2 * hid_units :]
    )
    stacked = jnp.concatenate([grad_gate, grad_up], axis=1)
    piece = lax.all_gather(stacked, "tok", axis=0, tiled=True)
    dx_part = dot_rows(piece[:, :hid_units], w_gate) + dot_rows(piece[:, hid_units:], w_up)
    quarter = val_count // lax.axis_size("hid")
    first_row = lax.axis_index("hid") * quarter
    dx_rows = lax.psum_scatter(dx_part, "hid", scatter_dimension=0, tiled=True)
    own_rows = lax.dynamic_slice_in_dim(val_out_grad, first_row, quarter, 0)
    val_grad = (own_rows.astype(jnp.float32) + dx_rows).astype(jnp.bfloat16)
    attn_full, grad_full = (
        lax.all_gather(val_attn_inputs, "tok", axis=1, tiled=True),
        lax.all_gather(val_grad, "tok", axis=1, tiled=True),
    )
    total = pair_terms(
        train_inputs,
        train_grads,
        lax.all_gather(attn_full, "hid", axis=0, tiled=True),
        lax.all_gather(grad_full, "hid", axis=0, tiled=True),
    )
    influence = total / (train_inputs.shape[1] * math.sqrt(val_count))
    return (influence, val_grad)


def solution(mesh):
    placed = (
        P(None, "tok"),
        P(None, "tok"),
        P("tok", "hid"),
        P("tok", "hid"),
        P("hid", "tok"),
        P("hid", "tok"),
        P(("hid", "tok"), None),
        P(("hid", "tok"), None),
    )
    return jax.shard_map(
        local,
        mesh=mesh,
        in_specs=placed,
        out_specs=(P(("hid", "tok")), P("hid", "tok")),
        check_vma=False,
    )
```

profile of v0, /device:TPU:1, one launch (start us, length us, event | category | flops | bytes accessed | tf_op | source)
XLA Modules:
  0.0 1299.6 jit_solution(1939003087148605138)
XLA Ops:
  7.3 1.8 fusion.13
  9.0 0.7 fusion.14
  9.7 0.7 fusion.15
  10.4 4.4 pad_maximum_fusion
  14.8 0.6 copy-done.7
  15.4 0.6 dynamic-slice
  16.7 697.3 %all-reduce.3.cloned.1.call-done = f32[256,10752]{1,0:T(8,128)} async-done(((f32[256,10752]{1,0:T(8,128)}), f32[256,10752]{1,0:T(8,128)}) %all-reduce.3.cloned.1.call-update) | async-done | bytes 11010064
  713.9 1.1 fusion.11
  715.1 0.6 maximum_bitcast_fusion
  715.8 0.1 copy.14
  715.9 162.7 %all-gather.9.cloned.1.call-done = bf16[64,4,7168]{2,1,0:T(4,128)(2,1)} async-done(((bf16[1,4,7168]{2,1,0:T(4,128)(2,1)}), bf16[64,4,7168]{2,1,0:T(4,128)(2,1)}) %all-gather.9.cloned.1.call-update) | async-done | bytes 3670032 | tf_op jit(solution)/shard_map/all_gather | solution.py:47
  878.6 6.7 reshape.5
  885.3 2.1 fusion
  887.4 2.8 fusion.6
  890.3 155.9 %all_gather.15 = bf16[64,4096]{0,1:T(8,128)(2,1)S(1)} all-gather(bf16[64,64]{0,1:T(8,128)(2,1)S(1)} %copy.14), channel_id=1, replica_groups=mesh['hid'=4,'tok'=64] {'tok'}, dimensions={1}, use_global_device_ids=true | all-gather | bytes 532480 | tf_op jit(solution)/shard_map/all_gather | solution.py:55
  1046.2 1.1 copy.15
  1047.5 0.1 copy.19
  1047.6 0.8 add_convert_fusion
  1048.4 153.2 %all_gather.18 = bf16[64,4096]{0,1:T(8,128)(2,1)S(1)} all-gather(bf16[64,64]{0,1:T(8,128)(2,1)S(1)} %copy.17), channel_id=1, replica_groups=mesh['hid'=4,'tok'=64] {'tok'}, dimensions={1}, use_global_device_ids=true | all-gather | bytes 532480 | tf_op jit(solution)/shard_map/all_gather | solution.py:56
  1201.7 1.1 copy.18
  1202.9 5.0 fusion.12
  1207.9 79.7 %all-gather.7.cloned.1.call-done = bf16[256,4096]{1,0:T(8,128)(2,1)} async-done(((bf16[64,4096]{1,0:T(8,128)(2,1)}), bf16[256,4096]{1,0:T(8,128)(2,1)}) %all-gather.7.cloned.1.call-update) | async-done | bytes 2097168 | tf_op jit(solution)/shard_map/all_gather | solution.py:62
  1287.5 5.0 fusion.5
  1292.5 0.6 broadcast_multiply_fusion
  (29 shorter events, 0.5 us)
Async XLA Ops:
  7.2 1.9 copy-start
  7.2 1.8 copy-start.3
  7.2 2.5 copy-start.1
  7.2 2.5 copy-start.4
  7.2 706.7 %all-reduce.3.cloned.1.call-start = ((), (), s32[]{:S(2)}) async-start(), calls=%async_computation.5 | async-start | bytes 22020096
  14.8 0.7 copy-start.7
  14.8 701.0 %copy-start.6 = (bf16[64,64]{1,0:T(8,128)(2,1)S(1)}, bf16[64,64]{1,0:T(8,128)(2,1)}, u32[]{:S(2)}) copy-start(bf16[64,64]{1,0:T(8,128)(2,1)} %param.13) | copy-start | bytes 24580
  14.8 863.8 %all-gather.9.cloned.1.call-start = ((), (), s32[]{:S(2)}) async-start(), calls=%async_computation.4 | async-start | bytes 3727360 | tf_op jit(solution)/shard_map/all_gather | solution.py:47
  715.7 331.8 %reduce-scatter.2.cloned.1.call-start = ((), (), s32[]{:S(2)}) async-start(), calls=%async_computation.2 | async-start | bytes 163840 | tf_op jit(solution)/shard_map/reduce_scatter | solution.py:51
  715.9 171.5 %copy-start.2 = (bf16[64,3584]{1,0:T(8,128)(2,1)S(1)}, bf16[64,3584]{1,0:T(8,128)(2,1)}, u32[]{:S(2)}) copy-start(bf16[64,3584]{1,0:T(8,128)(2,1)} %param.10) | copy-start | bytes 1376260
  890.2 312.6 %all-gather.5.cloned.1.call-start = ((), (), s32[]{:S(2)}) async-start(), calls=%async_computation.1 | async-start | bytes 2621440 | tf_op jit(solution)/shard_map/all_gather | solution.py:61
  1047.3 240.2 %all-gather.7.cloned.1.call-start = ((), (), s32[]{:S(2)}) async-start(), calls=%async_computation.3 | async-start | bytes 2621440 | tf_op jit(solution)/shard_map/all_gather | solution.py:62
  1048.4 159.5 %copy-start.5 = (bf16[64,64]{1,0:T(8,128)(2,1)}, bf16[64,64]{1,0:T(8,128)(2,1)S(1)}, u32[]{:S(2)}) copy-start(bf16[64,64]{1,0:T(8,128)(2,1)S(1)} %add_convert_fusion) | copy-start | bytes 24580
Sparse Core Ops, SparseCore 0:
  14.9 698.9 all-reduce.2
  717.4 161.1 all-gather.8
  890.4 20.3 reduce-scatter.1
  1047.4 56.4 all-gather.4
  1203.0 84.5 all-gather.6
where the time goes:
time: 1300 us
  waiting for transfers between devices  940 us (72%)
  blocking collectives  309 us (24%)
  matrix products  17.9 us (1%)
  between operations  14.6 us (1%)
    unnamed x6, waiting for transfers between devices  697 us
    all_gather x1, waiting for transfers between devices, local(): piece = lax.all_gather(stacked, 'tok', axis=0, tiled=True)  163 us
    all_gather x1, blocking collectives, local(): lax.all_gather(val_attn_inputs, 'tok', axis=1, tiled=True)  156 us
    all_gather x1, blocking collectives, local(): lax.all_gather(val_grad, 'tok', axis=1, tiled=True)  153 us
    all_gather x1, waiting for transfers between devices, local(): lax.all_gather(grad_full, 'hid', axis=0, tiled=True)  79.7 us
  transfers between devices with their start and end apart: 5, of which 3 were waited for; matrix products, arithmetic and copies ran while one was open for 1% of the time, Pallas kernels for 0%

commit v1 on v0

--- a/solution.py
+++ b/solution.py
@@ -29,6 +29,13 @@
 def local(
     val_inputs, val_out_grad, w_gate, w_up, w_down, val_attn_inputs, train_inputs, train_grads
 ):
+
+    def floor_watch(page):
+        vec_out = jnp.concatenate(
+            lax.all_to_all(jnp.stack([page] * lax.axis_size("tok")), "tok", 0, 0), 1
+        )
+        return vec_out
+
     hid_units = w_gate.shape[1]
     val_count = val_out_grad.shape[0]
     gate_pre = jnp.dot(val_inputs, w_gate, preferred_element_type=jnp.float32)
@@ -53,7 +60,7 @@
     val_grad = (own_rows.astype(jnp.float32) + dx_rows).astype(jnp.bfloat16)
     attn_full, grad_full = (
         lax.all_gather(val_attn_inputs, "tok", axis=1, tiled=True),
-        lax.all_gather(val_grad, "tok", axis=1, tiled=True),
+        floor_watch(val_grad),
     )
     total = pair_terms(
         train_inputs,

time: 1300 us -> 1150 us (0.88)
  blocking collectives: 309 us -> 175 us
  waiting for transfers between devices: 940 us -> 925 us
    all_gather x1 -> x0, blocking collectives: 153 us -> none  [local(): lax.all_gather(val_grad, 'tok', axis=1, tiled=True)]
    all_gather x1, waiting for transfers between devices: 79.7 us -> 29.2 us  [local(): lax.all_gather(grad_full, 'hid', axis=0, tiled=True)]
    all_gather x1, waiting for transfers between devices: 0.02 us -> 36.1 us  [local(): lax.all_gather(attn_full, 'hid', axis=0, tiled=True)]
    all_to_all x0 -> x1, blocking collectives: none -> 19.4 us  [floor_watch(): lax.all_to_all(jnp.stack([page] * lax.axis_size('tok')), 'tok', 0, 0)]
  transfers between devices with their start and end apart: 5 -> 5, of which waited for: 3 -> 4; matrix products, arithmetic and copies ran while one was open for 1% -> 1% of each run, Pallas kernels for 0% -> 0%
where the time goes in v1:
time: 1150 us
  waiting for transfers between devices  925 us (80%)
  blocking collectives  175 us (15%)
  matrix products  17.9 us (2%)
  between operations  14.6 us (1%)
  local copies, waits for them, and re-layouts  13.3 us (1%)
    unnamed x6, waiting for transfers between devices  697 us
    all_gather x1, waiting for transfers between devices, local(): piece = lax.all_gather(stacked, 'tok', axis=0, tiled=True)  163 us
    all_gather x1, blocking collectives, local(): lax.all_gather(val_attn_inputs, 'tok', axis=1, tiled=True)  156 us
    all_gather x1, waiting for transfers between devices, local(): lax.all_gather(attn_full, 'hid', axis=0, tiled=True)  36.1 us
    all_gather x1, waiting for transfers between devices, local(): lax.all_gather(grad_full, 'hid', axis=0, tiled=True)  29.2 us
  transfers between devices with their start and end apart: 5, of which 4 were waited for; matrix products, arithmetic and copies ran while one was open for 1% of the time, Pallas kernels for 0%

profile of v1, /device:TPU:1, one launch (start us, length us, event | category | flops | bytes accessed | tf_op | source)
XLA Modules:
  0.0 1154.2 jit_solution(1551896054513896411)
XLA Ops:
  7.3 1.8 fusion.13
  9.0 0.7 fusion.14
  9.7 0.7 fusion.15
  10.4 4.4 pad_maximum_fusion
  14.8 0.6 copy-done.7
  16.7 697.3 %all-reduce.3.cloned.1.call-done = f32[256,10752]{1,0:T(8,128)} async-done(((f32[256,10752]{1,0:T(8,128)}), f32[256,10752]{1,0:T(8,128)}) %all-reduce.3.cloned.1.call-update) | async-done | bytes 11010064
  713.9 1.1 fusion.11
  715.1 0.6 maximum_bitcast_fusion
  715.9 162.7 %all-gather.9.cloned.1.call-done = bf16[64,4,7168]{2,1,0:T(4,128)(2,1)} async-done(((bf16[1,4,7168]{2,1,0:T(4,128)(2,1)}), bf16[64,4,7168]{2,1,0:T(4,128)(2,1)}) %all-gather.9.cloned.1.call-update) | async-done | bytes 3670032 | tf_op jit(solution)/shard_map/all_gather | solution.py:54
  878.6 6.7 reshape.15
  885.3 2.1 fusion
  887.4 2.8 fusion.6
  890.3 155.9 %all_gather.12 = bf16[64,4096]{0,1:T(8,128)(2,1)S(1)} all-gather(bf16[64,64]{0,1:T(8,128)(2,1)S(1)} %copy.15), channel_id=1, replica_groups=mesh['hid'=4,'tok'=64] {'tok'}, dimensions={1}, use_global_device_ids=true | all-gather | bytes 532480 | tf_op jit(solution)/shard_map/all_gather | solution.py:62
  1046.2 1.1 copy.16
  1047.6 0.8 add_convert_fusion
  1048.6 0.7 reshape.17
  1049.3 19.4 %all_to_all.5 = bf16[64,2,2048]{2,1,0:T(2,128)(2,1)S(1)} all-to-all(bf16[64,2,2048]{2,1,0:T(2,128)(2,1)S(1)} %reshape.17), channel_id=1, replica_groups=mesh['hid'=4,'tok'=64] {'tok'}, dimensions={0} | all-to-all | bytes 1048576 | tf_op jit(solution)/shard_map/all_to_all | solution.py:35
  1068.7 0.7 reshape.18
  1069.4 0.7 copy.18
  1070.1 1.6 reshape.13
  1071.8 36.1 %all-gather.5.cloned.1.call-done = bf16[256,4096]{1,0:T(8,128)(2,1)} async-done(((bf16[64,4096]{1,0:T(8,128)(2,1)}), bf16[256,4096]{1,0:T(8,128)(2,1)}) %all-gather.5.cloned.1.call-update) | async-done | bytes 2097168 | tf_op jit(solution)/shard_map/all_gather | solution.py:68
  1107.9 5.0 fusion.12
  1112.9 29.2 %all-gather.7.cloned.1.call-done = bf16[256,4096]{1,0:T(8,128)(2,1)} async-done(((bf16[64,4096]{1,0:T(8,128)(2,1)}), bf16[256,4096]{1,0:T(8,128)(2,1)}) %all-gather.7.cloned.1.call-update) | async-done | bytes 2097168 | tf_op jit(solution)/shard_map/all_gather | solution.py:69
  1142.1 5.0 fusion.5
  (32 shorter events, 2.0 us)
Async XLA Ops:
  7.2 1.9 copy-start
  7.2 1.8 copy-start.3
  7.2 2.5 copy-start.1
  7.2 2.5 copy-start.4
  7.2 706.7 %all-reduce.3.cloned.1.call-start = ((), (), s32[]{:S(2)}) async-start(), calls=%async_computation.6 | async-start | bytes 22020096
  14.8 0.7 copy-start.7
  14.8 701.0 %copy-start.6 = (bf16[64,64]{1,0:T(8,128)(2,1)S(1)}, bf16[64,64]{1,0:T(8,128)(2,1)}, u32[]{:S(2)}) copy-start(bf16[64,64]{1,0:T(8,128)(2,1)} %param.13) | copy-start | bytes 24580
  14.8 863.8 %all-gather.9.cloned.1.call-start = ((), (), s32[]{:S(2)}) async-start(), calls=%async_computation.5 | async-start | bytes 3727360 | tf_op jit(solution)/shard_map/all_gather | solution.py:54
  715.7 331.8 %reduce-scatter.2.cloned.1.call-start = ((), (), s32[]{:S(2)}) async-start(), calls=%async_computation.3 | async-start | bytes 163840 | tf_op jit(solution)/shard_map/reduce_scatter | solution.py:58
  715.9 171.5 %copy-start.2 = (bf16[64,3584]{1,0:T(8,128)(2,1)S(1)}, bf16[64,3584]{1,0:T(8,128)(2,1)}, u32[]{:S(2)}) copy-start(bf16[64,3584]{1,0:T(8,128)(2,1)} %param.10) | copy-start | bytes 1376260
  890.2 217.7 %all-gather.5.cloned.1.call-start = ((), (), s32[]{:S(2)}) async-start(), calls=%async_computation.2 | async-start | bytes 2621440 | tf_op jit(solution)/shard_map/all_gather | solution.py:68
  1047.3 94.8 %all-gather.7.cloned.1.call-start = ((), (), s32[]{:S(2)}) async-start(), calls=%async_computation.4 | async-start | bytes 2621440 | tf_op jit(solution)/shard_map/all_gather | solution.py:69
  1048.4 21.8 %copy-start.5 = (bf16[64,64]{1,0:T(8,128)(2,1)}, bf16[64,64]{1,0:T(8,128)(2,1)S(1)}, u32[]{:S(2)}) copy-start(bf16[64,64]{1,0:T(8,128)(2,1)S(1)} %add_convert_fusion) | copy-start | bytes 24580
Sparse Core Ops, SparseCore 0:
  14.9 698.9 all-reduce.2
  717.4 161.1 all-gather.8
  890.4 20.3 reduce-scatter.1
  1047.4 60.4 all-gather.4
  1109.6 32.5 all-gather.6

commit v2 on v0

--- a/solution.py
+++ b/solution.py
@@ -51,8 +51,13 @@
     dx_rows = lax.psum_scatter(dx_part, "hid", scatter_dimension=0, tiled=True)
     own_rows = lax.dynamic_slice_in_dim(val_out_grad, first_row, quarter, 0)
     val_grad = (own_rows.astype(jnp.float32) + dx_rows).astype(jnp.bfloat16)
+
+    def measure_cycles(incoming_x, axis_no):
+        row_out = lax.all_gather(incoming_x, axis_name="tok")
+        return jnp.concatenate(row_out, axis=axis_no)
+
     attn_full, grad_full = (
-        lax.all_gather(val_attn_inputs, "tok", axis=1, tiled=True),
+        measure_cycles(val_attn_inputs, axis_no=1),
         lax.all_gather(val_grad, "tok", axis=1, tiled=True),
     )
     total = pair_terms(

time: 1300 us -> 1300 us (level)
  no operation moved by 1% of the time
where the time goes in v2:
time: 1300 us
  waiting for transfers between devices  941 us (72%)
  blocking collectives  308 us (24%)
  matrix products  17.9 us (1%)
  between operations  14.6 us (1%)
    unnamed x6, waiting for transfers between devices  697 us
    all_gather x1, waiting for transfers between devices, local(): piece = lax.all_gather(stacked, 'tok', axis=0, tiled=True)  163 us
    all_gather x1, blocking collectives, measure_cycles(): row_out = lax.all_gather(incoming_x, axis_name='tok')  156 us
    all_gather x1, blocking collectives, local(): lax.all_gather(val_grad, 'tok', axis=1, tiled=True)  152 us
    all_gather x1, waiting for transfers between devices, local(): lax.all_gather(grad_full, 'hid', axis=0, tiled=True)  80.4 us
  transfers between devices with their start and end apart: 5, of which 3 were waited for; matrix products, arithmetic and copies ran while one was open for 1% of the time, Pallas kernels for 0%

profile of v2, /device:TPU:1, one launch (start us, length us, event | category | flops | bytes accessed | tf_op | source)
XLA Modules:
  0.0 1300.8 jit_solution(13691281668593831053)
XLA Ops:
  7.3 1.8 fusion.13
  9.0 0.7 fusion.14
  9.7 0.7 fusion.15
  10.4 4.4 pad_maximum_fusion
  14.8 0.6 copy-done.7
  15.4 0.6 dynamic-slice
  16.7 697.3 %all-reduce.3.cloned.1.call-done = f32[256,10752]{1,0:T(8,128)} async-done(((f32[256,10752]{1,0:T(8,128)}), f32[256,10752]{1,0:T(8,128)}) %all-reduce.3.cloned.1.call-update) | async-done | bytes 11010064
  713.9 1.1 fusion.11
  715.1 0.6 maximum_bitcast_fusion
  715.8 162.8 %all-gather.10.cloned.1.call-done = bf16[64,4,7168]{2,1,0:T(4,128)(2,1)} async-done(((bf16[1,4,7168]{2,1,0:T(4,128)(2,1)}), bf16[64,4,7168]{2,1,0:T(4,128)(2,1)}) %all-gather.10.cloned.1.call-update) | async-done | bytes 3670032 | tf_op jit(solution)/shard_map/all_gather | solution.py:47
  878.6 6.7 reshape.14
  885.3 2.1 fusion
  887.5 2.8 fusion.6
  890.3 155.9 %all-gather = bf16[4096,64]{1,0:T(8,128)(2,1)S(1)} all-gather(bf16[64,64]{1,0:T(8,128)(2,1)S(1)} %copy-done.6), channel_id=2, replica_groups=mesh['hid'=4,'tok'=64] {'tok'}, dimensions={0}, use_global_device_ids=true | all-gather | bytes 532480 | tf_op jit(solution)/shard_map/all_gather | solution.py:56
  1046.2 0.7 copy.22
  1046.9 1.6 reshape.11
  1048.7 0.1 copy.20
  1048.8 0.8 add_convert_fusion
  1049.7 152.4 %all_gather.22 = bf16[64,4096]{0,1:T(8,128)(2,1)S(1)} all-gather(bf16[64,64]{0,1:T(8,128)(2,1)S(1)} %copy.18), channel_id=1, replica_groups=mesh['hid'=4,'tok'=64] {'tok'}, dimensions={1}, use_global_device_ids=true | all-gather | bytes 532480 | tf_op jit(solution)/shard_map/all_gather | solution.py:61
  1202.1 1.1 copy.19
  1203.3 5.0 fusion.12
  1208.3 80.4 %all-gather.8.cloned.1.call-done = bf16[256,4096]{1,0:T(8,128)(2,1)} async-done(((bf16[64,4096]{1,0:T(8,128)(2,1)}), bf16[256,4096]{1,0:T(8,128)(2,1)}) %all-gather.8.cloned.1.call-update) | async-done | bytes 2097168 | tf_op jit(solution)/shard_map/all_gather | solution.py:67
  1288.7 5.0 fusion.5
  1293.7 0.6 broadcast_multiply_fusion
  (29 shorter events, 0.5 us)
Async XLA Ops:
  7.2 1.9 copy-start
  7.2 1.8 copy-start.3
  7.2 2.5 copy-start.1
  7.2 2.5 copy-start.4
  7.2 706.7 %all-reduce.3.cloned.1.call-start = ((), (), s32[]{:S(2)}) async-start(), calls=%async_computation.5 | async-start | bytes 22020096
  14.8 0.7 copy-start.7
  14.8 863.8 %all-gather.10.cloned.1.call-start = ((), (), s32[]{:S(2)}) async-start(), calls=%async_computation.4 | async-start | bytes 3727360 | tf_op jit(solution)/shard_map/all_gather | solution.py:47
  715.7 171.7 %copy-start.2 = (bf16[64,3584]{1,0:T(8,128)(2,1)S(1)}, bf16[64,3584]{1,0:T(8,128)(2,1)}, u32[]{:S(2)}) copy-start(bf16[64,3584]{1,0:T(8,128)(2,1)} %param.10) | copy-start | bytes 1376260
  715.8 333.0 %reduce-scatter.2.cloned.1.call-start = ((), (), s32[]{:S(2)}) async-start(), calls=%async_computation.2 | async-start | bytes 163840 | tf_op jit(solution)/shard_map/reduce_scatter | solution.py:51
  885.3 5.0 copy-start.6
  890.3 313.0 %all-gather.6.cloned.1.call-start = ((), (), s32[]{:S(2)}) async-start(), calls=%async_computation.1 | async-start | bytes 2621440 | tf_op jit(solution)/shard_map/all_gather | solution.py:66
  1048.5 240.2 %all-gather.8.cloned.1.call-start = ((), (), s32[]{:S(2)}) async-start(), calls=%async_computation.3 | async-start | bytes 2621440 | tf_op jit(solution)/shard_map/all_gather | solution.py:67
  1049.6 158.7 %copy-start.5 = (bf16[64,64]{1,0:T(8,128)(2,1)}, bf16[64,64]{1,0:T(8,128)(2,1)S(1)}, u32[]{:S(2)}) copy-start(bf16[64,64]{1,0:T(8,128)(2,1)S(1)} %add_convert_fusion) | copy-start | bytes 24580
Sparse Core Ops, SparseCore 0:
  14.9 698.9 all-reduce.2
  717.4 161.1 all-gather.9
  890.4 20.3 reduce-scatter.1
  1048.7 56.4 all-gather.5
  1203.4 85.2 all-gather.7
